TPU v7x, 32 devices: a whole 2x2x4 slice. The times are simulated.
32 devices in a mesh: section: 2 (over x), req: 8 (over z, y), head: 2 (over core).
Axes of the slice: x: 2, y: 2, z: 4, core: 2. Of those that a mesh axis runs over, the one named last changes fastest.
Arguments:
- latent_tokens: bfloat16 [8, 2, 256, 1536], P('req', None, 'head'), may hold values from -6 to 6
- w_qkv: bfloat16 [2, 1536, 4608], P('section', 'req', 'head'), may hold values from -0.15625 to 0.15625
- w_out: bfloat16 [2, 1536, 1536], P('section', 'head', 'req'), may hold values from -0.75 to 0.75
- time_mod: float32 [2, 28, 3, 1536], P('section'), may hold values from -3 to 3
- text_mod: float32 [2, 8, 2, 3, 1536], P('section', 'req'), may hold values from -3 to 3
- stale_kv: bfloat16 [2, 8, 2, 1178, 3072], P('section', 'req', None, None, 'head'), may hold values from -150 to 150
- guided: int32 [8], P('req'), may hold values 0 or 1
- patch_index: int32 [8], P('req'), may hold values from 0 to 3
- timestep: int32 [8], P('req'), may hold values from 0 to 27
Outputs:
- hidden_out: bfloat16 [2, 8, 2, 256, 1536], P('section', 'req', None, 'head')
- fresh_kv: bfloat16 [2, 8, 2, 256, 3072], P('section', 'req', None, None, 'head')
All inputs are finite; a program needn't handle non-finite values. No bound on the sum of `guided` on one device may be relied on, other than what follows from the above.
Results may differ from a plain program's by a relative error of at most 0.04.
Values may be sent and summed in bfloat16 or wider, within the bound.
A program may use at most 192 MiB of HBM per device.

v0:
```python
import jax
import jax.numpy as jnp
from jax import lax
from jax.sharding import PartitionSpec as P

HD = 64
PATCH = 256
PATCHES = 4
STALE = 1178


def shifted(block, axis, distance):
    devices = range(lax.axis_size(axis))
    route = [(i - distance, i) for i in devices if i - distance in devices]
    return lax.ppermute(block, axis, route)


def attend(queries, own_keys, own_values, stale_pair, patch_here):
    heads_here = queries.shape[1]
    stale_split = stale_pair.reshape(STALE, heads_here, 2, HD)
    stale_keys = stale_split[:, :, 0]
    stale_values = stale_split[:, :, 1]
    all_keys = jnp.concatenate([own_keys, stale_keys], 0)
    all_values = jnp.concatenate([own_values, stale_values], 0)
    scores = jnp.einsum(
        "qhd,khd->hqk", queries, all_keys, preferred_element_type=jnp.float32
    ) * HD ** (-0.5)
    position = jnp.arange(PATCH + STALE, dtype=jnp.int32)
    stale_pos = position - PATCH
    hidden_key = (
        (stale_pos >= 0) & (stale_pos < PATCHES * PATCH) & (stale_pos // PATCH == patch_here)
    )
    scores = jnp.where(hidden_key[None, None, :], -jnp.inf, scores)
    row_max = jnp.max(scores, axis=-1, keepdims=True)
    exponent = jnp.exp(scores - row_max)
    weights = (exponent / jnp.sum(exponent, axis=-1, keepdims=True)).astype(jnp.bfloat16)
    mixed_heads = jnp.einsum(
        "hqk,khd->qhd", weights, all_values, preferred_element_type=jnp.float32
    )
    return mixed_heads.astype(jnp.bfloat16).reshape(PATCH, heads_here * HD)


def shards(
    latent_tokens, w_qkv, w_out, time_mod, text_mod, stale_kv, guided, patch_index, timestep
):
    section_index = lax.axis_index("section")
    requests = latent_tokens.shape[0]
    item_count = 2 * requests
    local_rows = latent_tokens.shape[2]
    model_width = latent_tokens.shape[3]
    pair_cols = stale_kv.shape[-1]
    feature_cols = pair_cols // 2
    heads_here = feature_cols // HD
    table_rows = time_mod.shape[1]
    tokens = latent_tokens.reshape(item_count, local_rows, model_width)
    picker = (timestep[:, None] == jnp.arange(table_rows, dtype=jnp.int32)[None, :]).astype(
        jnp.float32
    )
    per_time = jnp.einsum("rt,tcd->rcd", picker, time_mod[0], precision=lax.Precision.HIGHEST)
    modulation = (per_time[:, None] + text_mod[0]).reshape(item_count, 3, model_width)
    stale_all = stale_kv[0].reshape(item_count, STALE, pair_cols)
    patch_all = jnp.repeat(patch_index, 2)
    guided_all = jnp.repeat(guided, 2)
    parity = jnp.arange(item_count, dtype=jnp.int32) % 2
    keep_all = jnp.where((parity == 1) & (guided_all == 0), 0.0, 1.0).astype(jnp.float32)
    qkv_full, out_full = (
        lax.all_gather(w_qkv[0], "req", axis=0, tiled=True),
        lax.all_gather(w_out[0], "req", axis=1, tiled=True),
    )

    def project_in(normed):
        return jnp.dot(normed, qkv_full, preferred_element_type=jnp.float32)

    def project_out(mixed_heads):
        return jnp.dot(mixed_heads, out_full, preferred_element_type=jnp.float32)

    def tick_step(tick_index, state_tuple):
        sent, hidden_buf, fresh_buf = state_tuple
        received = shifted(sent, "section", 1)
        item_index = tick_index - section_index
        in_range = (item_index >= 0) & (item_index < item_count)
        slot_index = jnp.clip(item_index, 0, item_count - 1)
        own_tokens = lax.dynamic_index_in_dim(tokens, slot_index, 0, keepdims=False)
        layer_in = jnp.where(section_index == 0, own_tokens, received)
        gathered = lax.all_gather(layer_in, "head", axis=0, tiled=True)
        mod_here = lax.dynamic_index_in_dim(modulation, slot_index, 0, keepdims=False)
        values_f = gathered.astype(jnp.float32)
        row_mean = jnp.mean(values_f, axis=-1, keepdims=True)
        centered = values_f - row_mean
        row_var = jnp.mean(centered * centered, axis=-1, keepdims=True)
        normed = (centered * lax.rsqrt(row_var + 1e-06) * (1.0 + mod_here[1]) + mod_here[0]).astype(
            jnp.bfloat16
        )
        projected = project_in(normed).reshape(PATCH, heads_here, 3, HD)
        queries = projected[:, :, 0].astype(jnp.bfloat16)
        own_keys = projected[:, :, 1].astype(jnp.bfloat16)
        own_values = projected[:, :, 2].astype(jnp.bfloat16)
        stale_pair = lax.dynamic_index_in_dim(stale_all, slot_index, 0, keepdims=False)
        patch_here = lax.dynamic_index_in_dim(patch_all, slot_index, 0, keepdims=False)
        keep_here = lax.dynamic_index_in_dim(keep_all, slot_index, 0, keepdims=False)
        mixed_heads = attend(queries, own_keys, own_values, stale_pair, patch_here)
        out_terms = project_out(mixed_heads)
        attn_part = lax.psum_scatter(
            out_terms.astype(jnp.bfloat16), "head", scatter_dimension=0, tiled=True
        ).astype(jnp.float32)
        updated = (layer_in.astype(jnp.float32) + mod_here[2] * attn_part).astype(jnp.bfloat16)
        kept_rows = (updated.astype(jnp.float32) * keep_here).astype(jnp.bfloat16)
        previous = lax.dynamic_index_in_dim(hidden_buf, slot_index, 0, keepdims=False)
        stored_rows = jnp.where(in_range, kept_rows, previous)
        hidden_buf = lax.dynamic_update_index_in_dim(hidden_buf, stored_rows, slot_index, 0)
        fresh_pair = jnp.stack([own_keys, own_values], axis=2).reshape(PATCH, pair_cols)
        kept_fresh = (fresh_pair.astype(jnp.float32) * keep_here).astype(jnp.bfloat16)
        previous_fresh = lax.dynamic_index_in_dim(fresh_buf, slot_index, 0, keepdims=False)
        stored_fresh = jnp.where(in_range, kept_fresh, previous_fresh)
        fresh_buf = lax.dynamic_update_index_in_dim(fresh_buf, stored_fresh, slot_index, 0)
        return (updated, hidden_buf, fresh_buf)

    start_state = (
        jnp.zeros((local_rows, model_width), jnp.bfloat16),
        jnp.zeros((item_count, local_rows, model_width), jnp.bfloat16),
        jnp.zeros((item_count, PATCH, pair_cols), jnp.bfloat16),
    )
    finished = lax.fori_loop(0, item_count + 1, tick_step, start_state)
    hidden_out = finished[1].reshape(1, requests, 2, local_rows, model_width)
    fresh_kv = finished[2].reshape(1, requests, 2, PATCH, pair_cols)
    return (hidden_out, fresh_kv)


def solution(mesh):
    in_specs = (
        P("req", None, "head", None),
        P("section", "req", "head"),
        P("section", "head", "req"),
        P("section", None, None, None),
        P("section", "req", None, None, None),
        P("section", "req", None, None, "head"),
        P("req"),
        P("req"),
        P("req"),
    )
    out_specs = (P("section", "req", None, "head", None), P("section", "req", None, None, "head"))
    return jax.shard_map(shards, mesh=mesh, in_specs=in_specs, out_specs=out_specs, check_vma=False)
```

profile of v0, /device:TPU:0, one launch (start us, length us, event | category | flops | bytes accessed | tf_op | source)
XLA Modules:
  0.0 409.9 jit_solution(2994836607392291890)
XLA Ops:
  8.7 20.0 %copy.38 = bf16[1,1,2,1178,1536]{3,4,2,1,0:T(8,128)(2,1)} copy(bf16[1,1,2,1178,1536]{4,2,3,1,0:T(2,128)(2,1)} %param.16) | data formatting | bytes 14475264 | tf_op args[5]
  31.7 33.3 %all-gather.7.cloned.1.call-done = bf16[1,768,1536]{1,2,0:T(8,128)(2,1)} async-done(((bf16[1,768,192]{1,2,0:T(8,128)(2,1)}), bf16[1,768,1536]{1,2,0:T(8,128)(2,1)}) %all-gather.7.cloned.1.call-update) | async-done | bytes 2359312 | tf_op jit(solution)/shard_map/all_gather | solution.py:68
  65.0 4.3 %copy.39 = bf16[768,1536]{1,0:T(8,128)(2,1)} copy(bf16[768,1536]{0,1:T(8,128)(2,1)} %bitcast.102) | data formatting | bytes 4718592
  69.3 105.3 %all-gather.5.cloned.1.call-done = bf16[1,1536,2304]{2,1,0:T(8,128)(2,1)} async-done(((bf16[1,192,2304]{2,1,0:T(8,128)(2,1)}), bf16[1,1536,2304]{2,1,0:T(8,128)(2,1)}) %all-gather.5.cloned.1.call-update) | async-done | bytes 7077904 | tf_op jit(solution)/shard_map/all_gather | solution.py:67
  177.3 226.1 %while.20 = (s32[]{:T(128)}, bf16[128,1536]{1,0:T(8,128)(2,1)}, bf16[2,128,1536]{2,1,0:T(8,128)(2,1)}, bf16[2,256,1536]{2,1,0:T(8,128)(2,1)}, pred[]{:T(512)}, /...) while((s32[]{:T(128)}, bf16[128,1536]{1,0:T(8,128)(2,1)}, ...), condition=%wide.region_6.7_spmd.clone, body=%wide.region_0.6_spmd.clone.sunk | while | flops 3597972224 | bytes 154106176 | solution.py:123
  177.3 3.4 collective-permute-start
  180.7 2.4 constant_dynamic-slice_fusion.7
  189.7 2.4 all_gather.20
  192.6 6.1 %fusion.87 = bf16[256,2304]{0,1:T(8,128)(2,1)S(1)} fusion(bf16[1536,2304]{1,0:T(8,128)(2,1)} %get-tuple-element.539, bf16[256,1536]{1,0:T(8,128)(2,1)S(1)} %all_gather.20, f32[1536]{0:T(1024)S(1)} %get-tuple-element.484, f32[1536]{0:T(1024)S(1)} %get-tuple-element.485, f32[256]{0:T(256)S(1)} %add_rsqrt_fusion.2, f32[256]{0:T(256)S(1)} %broadcast_multiply_fusion.2), kind=kOutput, calls=%fused_computation.29.clone.1 | convolution fusion | flops 1814298624 | bytes 9058304 | tf_op jit(solution)/shard_map/while/body/eval_jaxpr/dot_general | solution.py:72
  198.8 8.5 %fusion.89 = f32[12,256,1434]{1,2,0:T(8,128)} fusion(bf16[1178,12,64]{0,2,1:T(8,128)(2,1)S(1)} %get-tuple-element.483, bf16[256,12,64]{0,2,1:T(8,128)(2,1)S(1)} %bitcast.95, bf16[256,12,1,64]{0,3,2,1:T(8,128)(2,1)S(1)} %get-tuple-element.487), kind=kOutput, calls=%fused_computation.13.clone.1 | convolution fusion | flops 568276992 | bytes 20216832 | tf_op jit(solution)/shard_map/while/body/eval_jaxpr/qhd,khd->hqk/dot_general | solution.py:25
  207.4 21.2 %fusion.91 = (f32[12,256]{1,0:T(8,128)}, f32[12,256,1434]{1,2,0:T(8,128)}) fusion(f32[12,256,1434]{1,2,0:T(8,128)} %fusion.89, pred[1434]{0:T(1024)(128)(4,1)S(1)} %fusion.90), kind=kOutput, calls=%fused_computation.86.clone.1 | output fusion | flops 26432920 | bytes 35255704 | tf_op jit(solution)/shard_map/while/body/eval_jaxpr/sub | solution.py:35
  228.6 7.9 %fusion.92 = bf16[12,64,256]{2,1,0:T(8,128)(2,1)S(1)} fusion(f32[12,256,1434]{1,2,0:T(8,128)} %get-tuple-element.488, f32[12,256]{1,0:T(8,128)} %get-tuple-element.489, bf16[1178,12,64]{0,2,1:T(8,128)(2,1)S(1)} %copy-done.1, bf16[256,12,64]{0,2,1:T(8,128)(2,1)S(1)} %bitcast.99), kind=kOutput, calls=%fused_computation.28.clone.1 | convolution fusion | flops 577284096 | bytes 20229120 | tf_op jit(solution)/shard_map/while/body/eval_jaxpr/hqk,khd->qhd/dot_general | solution.py:37
  243.5 2.8 reduce-scatter.2.cloned.1.call-done
  246.3 2.6 fusion.93
  250.8 3.6 collective-permute-start
  254.4 2.4 constant_dynamic-slice_fusion.7
  264.3 2.4 all_gather.20
  267.2 6.1 %fusion.87 = bf16[256,2304]{0,1:T(8,128)(2,1)S(1)} fusion(bf16[1536,2304]{1,0:T(8,128)(2,1)} %get-tuple-element.539, bf16[256,1536]{1,0:T(8,128)(2,1)S(1)} %all_gather.20, f32[1536]{0:T(1024)S(1)} %get-tuple-element.484, f32[1536]{0:T(1024)S(1)} %get-tuple-element.485, f32[256]{0:T(256)S(1)} %add_rsqrt_fusion.2, f32[256]{0:T(256)S(1)} %broadcast_multiply_fusion.2), kind=kOutput, calls=%fused_computation.29.clone.1 | convolution fusion | flops 1814298624 | bytes 9058304 | tf_op jit(solution)/shard_map/while/body/eval_jaxpr/dot_general | solution.py:72
  273.5 8.5 %fusion.89 = f32[12,256,1434]{1,2,0:T(8,128)} fusion(bf16[1178,12,64]{0,2,1:T(8,128)(2,1)S(1)} %get-tuple-element.483, bf16[256,12,64]{0,2,1:T(8,128)(2,1)S(1)} %bitcast.95, bf16[256,12,1,64]{0,3,2,1:T(8,128)(2,1)S(1)} %get-tuple-element.487), kind=kOutput, calls=%fused_computation.13.clone.1 | convolution fusion | flops 568276992 | bytes 20216832 | tf_op jit(solution)/shard_map/while/body/eval_jaxpr/qhd,khd->hqk/dot_general | solution.py:25
  282.0 21.2 %fusion.91 = (f32[12,256]{1,0:T(8,128)}, f32[12,256,1434]{1,2,0:T(8,128)}) fusion(f32[12,256,1434]{1,2,0:T(8,128)} %fusion.89, pred[1434]{0:T(1024)(128)(4,1)S(1)} %fusion.90), kind=kOutput, calls=%fused_computation.86.clone.1 | output fusion | flops 26432920 | bytes 35255704 | tf_op jit(solution)/shard_map/while/body/eval_jaxpr/sub | solution.py:35
  303.2 7.9 %fusion.92 = bf16[12,64,256]{2,1,0:T(8,128)(2,1)S(1)} fusion(f32[12,256,1434]{1,2,0:T(8,128)} %get-tuple-element.488, f32[12,256]{1,0:T(8,128)} %get-tuple-element.489, bf16[1178,12,64]{0,2,1:T(8,128)(2,1)S(1)} %copy-done.1, bf16[256,12,64]{0,2,1:T(8,128)(2,1)S(1)} %bitcast.99), kind=kOutput, calls=%fused_computation.28.clone.1 | convolution fusion | flops 577284096 | bytes 20229120 | tf_op jit(solution)/shard_map/while/body/eval_jaxpr/hqk,khd->qhd/dot_general | solution.py:37
  318.1 5.0 %reduce-scatter.2.cloned.1.call-done = bf16[128,1536]{1,0:T(8,128)(2,1)} async-done(((bf16[256,1536]{1,0:T(8,128)(2,1)}), bf16[128,1536]{1,0:T(8,128)(2,1)}) %reduce-scatter.2.cloned.1.call-update) | async-done | bytes 393232 | tf_op jit(solution)/shard_map/while/body/eval_jaxpr/reduce_scatter | solution.py:103
  323.1 2.6 fusion.93
  327.6 3.6 collective-permute-start
  331.2 2.4 constant_dynamic-slice_fusion.7
  341.1 2.4 all_gather.20
  344.0 6.1 %fusion.87 = bf16[256,2304]{0,1:T(8,128)(2,1)S(1)} fusion(bf16[1536,2304]{1,0:T(8,128)(2,1)} %get-tuple-element.539, bf16[256,1536]{1,0:T(8,128)(2,1)S(1)} %all_gather.20, f32[1536]{0:T(1024)S(1)} %get-tuple-element.484, f32[1536]{0:T(1024)S(1)} %get-tuple-element.485, f32[256]{0:T(256)S(1)} %add_rsqrt_fusion.2, f32[256]{0:T(256)S(1)} %broadcast_multiply_fusion.2), kind=kOutput, calls=%fused_computation.29.clone.1 | convolution fusion | flops 1814298624 | bytes 9058304 | tf_op jit(solution)/shard_map/while/body/eval_jaxpr/dot_general | solution.py:72
  350.3 8.5 %fusion.89 = f32[12,256,1434]{1,2,0:T(8,128)} fusion(bf16[1178,12,64]{0,2,1:T(8,128)(2,1)S(1)} %get-tuple-element.483, bf16[256,12,64]{0,2,1:T(8,128)(2,1)S(1)} %bitcast.95, bf16[256,12,1,64]{0,3,2,1:T(8,128)(2,1)S(1)} %get-tuple-element.487), kind=kOutput, calls=%fused_computation.13.clone.1 | convolution fusion | flops 568276992 | bytes 20216832 | tf_op jit(solution)/shard_map/while/body/eval_jaxpr/qhd,khd->hqk/dot_general | solution.py:25
  358.8 21.2 %fusion.91 = (f32[12,256]{1,0:T(8,128)}, f32[12,256,1434]{1,2,0:T(8,128)}) fusion(f32[12,256,1434]{1,2,0:T(8,128)} %fusion.89, pred[1434]{0:T(1024)(128)(4,1)S(1)} %fusion.90), kind=kOutput, calls=%fused_computation.86.clone.1 | output fusion | flops 26432920 | bytes 35255704 | tf_op jit(solution)/shard_map/while/body/eval_jaxpr/sub | solution.py:35
  380.0 7.9 %fusion.92 = bf16[12,64,256]{2,1,0:T(8,128)(2,1)S(1)} fusion(f32[12,256,1434]{1,2,0:T(8,128)} %get-tuple-element.488, f32[12,256]{1,0:T(8,128)} %get-tuple-element.489, bf16[1178,12,64]{0,2,1:T(8,128)(2,1)S(1)} %copy-done.1, bf16[256,12,64]{0,2,1:T(8,128)(2,1)S(1)} %bitcast.99), kind=kOutput, calls=%fused_computation.28.clone.1 | convolution fusion | flops 577284096 | bytes 20229120 | tf_op jit(solution)/shard_map/while/body/eval_jaxpr/hqk,khd->qhd/dot_general | solution.py:37
  394.9 5.0 %reduce-scatter.2.cloned.1.call-done = bf16[128,1536]{1,0:T(8,128)(2,1)} async-done(((bf16[256,1536]{1,0:T(8,128)(2,1)}), bf16[128,1536]{1,0:T(8,128)(2,1)}) %reduce-scatter.2.cloned.1.call-update) | async-done | bytes 393232 | tf_op jit(solution)/shard_map/while/body/eval_jaxpr/reduce_scatter | solution.py:103
  399.9 2.6 fusion.93
  (118 shorter events, 54.4 us)
Async XLA Ops:
  7.2 57.8 %all-gather.7.cloned.1.call-start = ((), (), s32[]{:S(2)}) async-start(), calls=%async_computation.2 | async-start | bytes 2654208 | tf_op jit(solution)/shard_map/all_gather | solution.py:68
  7.9 166.6 %all-gather.5.cloned.1.call-start = ((), (), s32[]{:S(2)}) async-start(), calls=%async_computation.1 | async-start | bytes 7962624 | tf_op jit(solution)/shard_map/all_gather | solution.py:67
  8.7 20.7 %copy-start.4 = (f32[1,28,3,1536]{3,0,2,1:T(1,128)S(1)}, f32[1,28,3,1536]{3,0,2,1:T(1,128)}, u32[]{:S(2)}) copy-start(f32[1,28,3,1536]{3,0,2,1:T(1,128)} %param.14) | copy-start | bytes 1548292
  8.7 22.3 %copy-start.5 = (f32[1,1,2,3,1536]{4,2,3,1,0:T(2,128)S(1)}, f32[1,1,2,3,1536]{4,2,3,1,0:T(2,128)}, u32[]{:S(2)}) copy-start(f32[1,1,2,3,1536]{4,2,3,1,0:T(2,128)} %param.15) | copy-start | bytes 110596
  177.3 69.0 %reduce-scatter.2.cloned.1.call-start = ((), (), s32[]{:S(2)}) async-start(), calls=%async_computation.3 | async-start | bytes 1179648 | tf_op jit(solution)/shard_map/while/body/eval_jaxpr/reduce_scatter | solution.py:103
  177.3 11.3 %collective-permute-start = (bf16[128,1536]{1,0:T(8,128)(2,1)S(1)}, bf16[128,1536]{1,0:T(8,128)(2,1)S(1)}, u32[]{:S(2)}, u32[]{:S(2)}) collective-permute-start(bf16[128,1536]{1,0:T(8,128)(2,1)S(1)} %broadcast_select_fusion.4), channel_id=1, source_target_pairs={{0,16},{1,17},{2,18},{3,19},{4,20},{5,21},{6,22},{7,23},{8,24},{9,... | collective-permute-start | bytes 1179656 | tf_op jit(solution)/shard_map/while/body/eval_jaxpr/ppermute | solution.py:15
  207.4 21.2 %copy-start.1 = (bf16[1178,12,64]{0,2,1:T(8,128)(2,1)S(1)}, bf16[1178,12,64]{0,2,1:T(8,128)(2,1)}, u32[]{:S(2)}) copy-start(bf16[1178,12,64]{0,2,1:T(8,128)(2,1)} %get-tuple-element.490) | copy-start | bytes 5428228 | tf_op jit(solution)/shard_map/while
  228.6 7.9 %copy-start = (bf16[768,1536]{1,0:T(8,128)(2,1)S(1)}, bf16[768,1536]{1,0:T(8,128)(2,1)}, u32[]{:S(2)}) copy-start(bf16[768,1536]{1,0:T(8,128)(2,1)} %get-tuple-element.542) | copy-start | bytes 7077892 | tf_op jit(solution)/shard_map/while
  242.2 4.0 copy-start.2
  248.9 0.9 copy-start.3
  249.7 73.4 %reduce-scatter.2.cloned.1.call-start = ((), (), s32[]{:S(2)}) async-start(), calls=%async_computation.3 | async-start | bytes 1179648 | tf_op jit(solution)/shard_map/while/body/eval_jaxpr/reduce_scatter | solution.py:103
  250.8 12.5 %collective-permute-start = (bf16[128,1536]{1,0:T(8,128)(2,1)S(1)}, bf16[128,1536]{1,0:T(8,128)(2,1)S(1)}, u32[]{:S(2)}, u32[]{:S(2)}) collective-permute-start(bf16[128,1536]{1,0:T(8,128)(2,1)S(1)} %broadcast_select_fusion.4), channel_id=1, source_target_pairs={{0,16},{1,17},{2,18},{3,19},{4,20},{5,21},{6,22},{7,23},{8,24},{9,... | collective-permute-start | bytes 1179656 | tf_op jit(solution)/shard_map/while/body/eval_jaxpr/ppermute | solution.py:15
  282.0 21.2 %copy-start.1 = (bf16[1178,12,64]{0,2,1:T(8,128)(2,1)S(1)}, bf16[1178,12,64]{0,2,1:T(8,128)(2,1)}, u32[]{:S(2)}) copy-start(bf16[1178,12,64]{0,2,1:T(8,128)(2,1)} %get-tuple-element.490) | copy-start | bytes 5428228 | tf_op jit(solution)/shard_map/while
  303.2 7.9 %copy-start = (bf16[768,1536]{1,0:T(8,128)(2,1)S(1)}, bf16[768,1536]{1,0:T(8,128)(2,1)}, u32[]{:S(2)}) copy-start(bf16[768,1536]{1,0:T(8,128)(2,1)} %get-tuple-element.542) | copy-start | bytes 7077892 | tf_op jit(solution)/shard_map/while
  316.9 6.3 %copy-start.2 = (bf16[2,128,1536]{2,1,0:T(8,128)(2,1)S(1)}, bf16[2,128,1536]{2,1,0:T(8,128)(2,1)}, u32[]{:S(2)}) copy-start(bf16[2,128,1536]{2,1,0:T(8,128)(2,1)} %get-tuple-element.515) | copy-start | bytes 2359300 | tf_op jit(solution)/shard_map/while
  325.7 0.9 copy-start.3
  326.6 73.3 %reduce-scatter.2.cloned.1.call-start = ((), (), s32[]{:S(2)}) async-start(), calls=%async_computation.3 | async-start | bytes 1179648 | tf_op jit(solution)/shard_map/while/body/eval_jaxpr/reduce_scatter | solution.py:103
  327.6 12.5 %collective-permute-start = (bf16[128,1536]{1,0:T(8,128)(2,1)S(1)}, bf16[128,1536]{1,0:T(8,128)(2,1)S(1)}, u32[]{:S(2)}, u32[]{:S(2)}) collective-permute-start(bf16[128,1536]{1,0:T(8,128)(2,1)S(1)} %broadcast_select_fusion.4), channel_id=1, source_target_pairs={{0,16},{1,17},{2,18},{3,19},{4,20},{5,21},{6,22},{7,23},{8,24},{9,... | collective-permute-start | bytes 1179656 | tf_op jit(solution)/shard_map/while/body/eval_jaxpr/ppermute | solution.py:15
  358.8 21.2 %copy-start.1 = (bf16[1178,12,64]{0,2,1:T(8,128)(2,1)S(1)}, bf16[1178,12,64]{0,2,1:T(8,128)(2,1)}, u32[]{:S(2)}) copy-start(bf16[1178,12,64]{0,2,1:T(8,128)(2,1)} %get-tuple-element.490) | copy-start | bytes 5428228 | tf_op jit(solution)/shard_map/while
  380.0 7.9 %copy-start = (bf16[768,1536]{1,0:T(8,128)(2,1)S(1)}, bf16[768,1536]{1,0:T(8,128)(2,1)}, u32[]{:S(2)}) copy-start(bf16[768,1536]{1,0:T(8,128)(2,1)} %get-tuple-element.542) | copy-start | bytes 7077892 | tf_op jit(solution)/shard_map/while
  393.7 6.2 %copy-start.2 = (bf16[2,128,1536]{2,1,0:T(8,128)(2,1)S(1)}, bf16[2,128,1536]{2,1,0:T(8,128)(2,1)}, u32[]{:S(2)}) copy-start(bf16[2,128,1536]{2,1,0:T(8,128)(2,1)} %get-tuple-element.515) | copy-start | bytes 2359300 | tf_op jit(solution)/shard_map/while
  402.5 0.9 copy-start.3
Sparse Core Ops, SparseCore 0:
  10.2 54.7 all-gather.6
  67.2 107.3 all-gather.4
  238.3 7.9 reduce-scatter.1
  312.9 10.1 reduce-scatter.1
  389.7 10.1 reduce-scatter.1
where the time goes:
time: 412 us; the launch traced here: 410 us
  waiting for transfers between devices  158 us (38%)
  other arithmetic  86.1 us (21%)
  matrix products  72.6 us (18%)
  local copies, waits for them, and re-layouts  59.1 us (14%)
  between operations  15.7 us (4%)
  starting transfers between devices  10.7 us (3%)
  blocking collectives  7.11 us (2%)
    all_gather x1, waiting for transfers between devices, shards(): lax.all_gather(w_qkv[0], 'req', axis=0, tiled=True)  105 us
    sub x3, other arithmetic, attend(): exponent = jnp.exp(scores - row_max)  63.7 us
    all_gather x1, waiting for transfers between devices, shards(): lax.all_gather(w_out[0], 'req', axis=1, tiled=True)  33.3 us
    dot_general x3, matrix products, attend(): jnp.einsum('qhd,khd->hqk', queries, all_keys, preferred_element_type=jnp....  25.5 us
    unnamed x6, local copies, waits for them, and re-layouts  24.3 us
    dot_general x3, matrix products, attend(): jnp.einsum('hqk,khd->qhd', weights, all_values, preferred_element_type=jn...  23.6 us
    dot_general x3, matrix products, project_in(): return jnp.dot(normed, qkv_full, preferred_element_type=jnp.float32)  18.2 us
    reduce_scatter x3, waiting for transfers between devices, tick_step(): lax.psum_scatter(out_terms.astype(jnp.bfloat16), 'head', scatter_dimensio...  12.8 us
  transfers between devices with their start and end apart: 8, of which 8 were waited for; matrix products, arithmetic and copies ran while one was open for 15% of the time, Pallas kernels for 0%

commit v1 on v0

--- a/solution.py
+++ b/solution.py
@@ -7,6 +7,23 @@
 PATCH = 256
 PATCHES = 4
 STALE = 1178
+
+
+def laid_out(blocks, dim):
+    blocks = jnp.moveaxis(blocks, 0, dim)
+    shape = blocks.shape
+    return blocks.reshape(*shape[:dim], shape[dim] * shape[dim + 1], *shape[dim + 2 :])
+
+
+def ring_gather(x, axis, dim):
+    peers = lax.axis_size(axis)
+    right = [(i, (i + 1) % peers) for i in range(peers)]
+    tiles = [x]
+    while len(tiles) < peers:
+        tiles.append(lax.ppermute(tiles[-1], axis, right))
+    position = lax.axis_index(axis)
+    tiles = jnp.stack(tiles)[(position - jnp.arange(peers)) % peers]
+    return laid_out(tiles, dim)
 
 
 def shifted(block, axis, distance):
@@ -64,7 +81,7 @@
     parity = jnp.arange(item_count, dtype=jnp.int32) % 2
     keep_all = jnp.where((parity == 1) & (guided_all == 0), 0.0, 1.0).astype(jnp.float32)
     qkv_full, out_full = (
-        lax.all_gather(w_qkv[0], "req", axis=0, tiled=True),
+        ring_gather(w_qkv[0], "req", 0),
         lax.all_gather(w_out[0], "req", axis=1, tiled=True),
     )
 

time: 412 us -> 430 us (1.044)
  local copies, waits for them, and re-layouts: 59.1 us -> 71.8 us
    ppermute x0 -> x7, waiting for transfers between devices: none -> 144 us  [ring_gather(): tiles.append(lax.ppermute(tiles[-1], axis, right))]
    all_gather x1 -> x0, waiting for transfers between devices: 105 us -> none  [shards(): lax.all_gather(w_qkv[0], 'req', axis=0, tiled=True)]
    all_gather x1, waiting for transfers between devices: 33.3 us -> 0.01 us  [shards(): lax.all_gather(w_out[0], 'req', axis=1, tiled=True)]
    unnamed x6 -> x11, local copies, waits for them, and re-layouts: 24.3 us -> 31.2 us
    gather x0 -> x1, local copies, waits for them, and re-layouts: none -> 6.81 us  [ring_gather(): tiles = jnp.stack(tiles)[(position - jnp.arange(peers)) % peers]]
  transfers between devices with their start and end apart: 8 -> 14, of which waited for: 8 -> 11; matrix products, arithmetic and copies ran while one was open for 15% -> 17% of each run, Pallas kernels for 0% -> 0%
where the time goes in v1:
time: 430 us; the launch traced here: 427 us
  waiting for transfers between devices  158 us (37%)
  other arithmetic  87.3 us (20%)
  matrix products  74.3 us (17%)
  local copies, waits for them, and re-layouts  71.8 us (17%)
  between operations  15.7 us (4%)
  starting transfers between devices  13.1 us (3%)
  blocking collectives  7.11 us (2%)
    ppermute x7, waiting for transfers between devices, ring_gather(): tiles.append(lax.ppermute(tiles[-1], axis, right))  144 us
    sub x3, other arithmetic, attend(): exponent = jnp.exp(scores - row_max)  63.7 us
    unnamed x11, local copies, waits for them, and re-layouts  31.2 us
    dot_general x3, matrix products, attend(): jnp.einsum('qhd,khd->hqk', queries, all_keys, preferred_element_type=jnp....  25.5 us
    dot_general x3, matrix products, attend(): jnp.einsum('hqk,khd->qhd', weights, all_values, preferred_element_type=jn...  23.6 us
    dot_general x3, matrix products, project_in(): return jnp.dot(normed, qkv_full, preferred_element_type=jnp.float32)  18.2 us
    reduce_scatter x3, waiting for transfers between devices, tick_step(): lax.psum_scatter(out_terms.astype(jnp.bfloat16), 'head', scatter_dimensio...  10 us
    ppermute x3, starting transfers between devices, shifted(): return lax.ppermute(block, axis, route)  9.99 us
  transfers between devices with their start and end apart: 14, of which 11 were waited for; matrix products, arithmetic and copies ran while one was open for 17% of the time, Pallas kernels for 0%

profile of v1, /device:TPU:0, one launch (start us, length us, event | category | flops | bytes accessed | tf_op | source)
XLA Modules:
  0.0 427.4 jit_solution(17489007910970302096)
XLA Ops:
  7.2 3.0 collective-permute-start.1
  10.2 22.9 %collective-permute-done.1 = bf16[192,2304]{1,0:T(8,128)(2,1)S(1)} collective-permute-done((bf16[192,2304]{1,0:T(8,128)(2,1)}, bf16[192,2304]{1,0:T(8,128)(2,1)S(1)}, u32[]{:S(2)}, u32[]{:S(2)}) %collective-permute-start.1) | collective-permute-done | bytes 884768 | tf_op jit(solution)/shard_map/ppermute | solution.py:23
  33.1 23.5 %collective-permute-done.2 = bf16[192,2304]{1,0:T(8,128)(2,1)S(1)} collective-permute-done((bf16[192,2304]{1,0:T(8,128)(2,1)S(1)}, bf16[192,2304]{1,0:T(8,128)(2,1)S(1)}, u32[]{:S(2)}, u32[]{:S(2)}) %collective-permute-start.2) | collective-permute-done | bytes 884768 | tf_op jit(solution)/shard_map/ppermute | solution.py:23
  59.3 20.0 %copy.38 = bf16[1,1,2,1178,1536]{3,4,2,1,0:T(8,128)(2,1)} copy(bf16[1,1,2,1178,1536]{4,2,3,1,0:T(2,128)(2,1)} %param.16) | data formatting | bytes 14475264 | tf_op args[5]
  81.4 8.3 %collective-permute-done.3 = bf16[192,2304]{1,0:T(8,128)(2,1)S(1)} collective-permute-done((bf16[192,2304]{1,0:T(8,128)(2,1)S(1)}, bf16[192,2304]{1,0:T(8,128)(2,1)S(1)}, u32[]{:S(2)}, u32[]{:S(2)}) %collective-permute-start.3) | collective-permute-done | bytes 884768 | tf_op jit(solution)/shard_map/ppermute | solution.py:23
  92.1 39.3 %collective-permute-done.4 = bf16[192,2304]{1,0:T(8,128)(2,1)S(1)} collective-permute-done((bf16[192,2304]{1,0:T(8,128)(2,1)S(1)}, bf16[192,2304]{1,0:T(8,128)(2,1)S(1)}, u32[]{:S(2)}, u32[]{:S(2)}) %collective-permute-start.4) | collective-permute-done | bytes 884768 | tf_op jit(solution)/shard_map/ppermute | solution.py:23
  133.4 19.5 %collective-permute-done.5 = bf16[192,2304]{1,0:T(8,128)(2,1)S(1)} collective-permute-done((bf16[192,2304]{1,0:T(8,128)(2,1)S(1)}, bf16[192,2304]{1,0:T(8,128)(2,1)S(1)}, u32[]{:S(2)}, u32[]{:S(2)}) %collective-permute-start.5) | collective-permute-done | bytes 884768 | tf_op jit(solution)/shard_map/ppermute | solution.py:23
  154.8 4.3 %copy.39 = bf16[768,1536]{1,0:T(8,128)(2,1)} copy(bf16[768,1536]{0,1:T(8,128)(2,1)} %bitcast.120) | data formatting | bytes 4718592
  159.1 16.3 %collective-permute-done.6 = bf16[192,2304]{1,0:T(8,128)(2,1)S(1)} collective-permute-done((bf16[192,2304]{1,0:T(8,128)(2,1)S(1)}, bf16[192,2304]{1,0:T(8,128)(2,1)S(1)}, u32[]{:S(2)}, u32[]{:S(2)}) %collective-permute-start.6) | collective-permute-done | bytes 884768 | tf_op jit(solution)/shard_map/ppermute | solution.py:23
  177.4 13.8 %collective-permute-done.7 = bf16[192,2304]{1,0:T(8,128)(2,1)S(1)} collective-permute-done((bf16[192,2304]{1,0:T(8,128)(2,1)S(1)}, bf16[192,2304]{1,0:T(8,128)(2,1)S(1)}, u32[]{:S(2)}, u32[]{:S(2)}) %collective-permute-start.7) | collective-permute-done | bytes 884768 | tf_op jit(solution)/shard_map/ppermute | solution.py:23
  192.1 6.8 %gather_fusion = bf16[8,192,2304]{2,1,0:T(8,128)(2,1)} fusion(bf16[8,192,2304]{2,1,0:T(8,128)(2,1)} %bitcast_dynamic-update-slice_fusion, s32[1024]{0:T(1024)S(1)} %pad_clamp_fusion), kind=kCustom, calls=%fused_computation | custom fusion | bytes 14155808 | tf_op jit(solution)/shard_map/gather | solution.py:25
  201.6 219.2 %while.20 = (s32[]{:T(128)}, bf16[128,1536]{1,0:T(8,128)(2,1)}, bf16[2,128,1536]{2,1,0:T(8,128)(2,1)}, bf16[2,256,1536]{2,1,0:T(8,128)(2,1)}, pred[]{:T(512)}, /...) while((s32[]{:T(128)}, bf16[128,1536]{1,0:T(8,128)(2,1)}, ...), condition=%wide.region_6.7_spmd.clone, body=%wide.region_0.6_spmd.clone.sunk | while | flops 3597972224 | bytes 147813120 | solution.py:140
  201.7 2.9 collective-permute-start
  215.4 6.1 %fusion.89 = bf16[256,2304]{0,1:T(8,128)(2,1)S(1)} fusion(bf16[1536,2304]{1,0:T(8,128)(2,1)} %get-tuple-element.539, bf16[256,1536]{1,0:T(8,128)(2,1)S(1)} %all_gather.16, f32[1536]{0:T(1024)S(1)} %get-tuple-element.484, f32[1536]{0:T(1024)S(1)} %get-tuple-element.485, f32[256]{0:T(256)S(1)} %add_rsqrt_fusion.2, f32[256]{0:T(256)S(1)} %broadcast_multiply_fusion.2), kind=kOutput, calls=%fused_computation.30.clone.1 | convolution fusion | flops 1814298624 | bytes 9058304 | tf_op jit(solution)/shard_map/while/body/eval_jaxpr/dot_general | solution.py:89
  221.6 8.5 %fusion.91 = f32[12,256,1434]{1,2,0:T(8,128)} fusion(bf16[1178,12,64]{0,2,1:T(8,128)(2,1)S(1)} %get-tuple-element.483, bf16[256,12,64]{0,2,1:T(8,128)(2,1)S(1)} %bitcast.112, bf16[256,12,1,64]{0,3,2,1:T(8,128)(2,1)S(1)} %get-tuple-element.487), kind=kOutput, calls=%fused_computation.14.clone.1 | convolution fusion | flops 568276992 | bytes 20216832 | tf_op jit(solution)/shard_map/while/body/eval_jaxpr/qhd,khd->hqk/dot_general | solution.py:42
  230.2 21.2 %fusion.93 = (f32[12,256]{1,0:T(8,128)}, f32[12,256,1434]{1,2,0:T(8,128)}) fusion(f32[12,256,1434]{1,2,0:T(8,128)} %fusion.91, pred[1434]{0:T(1024)(128)(4,1)S(1)} %fusion.92), kind=kOutput, calls=%fused_computation.102.clone.1 | output fusion | flops 26432920 | bytes 35255704 | tf_op jit(solution)/shard_map/while/body/eval_jaxpr/sub | solution.py:52
  251.4 7.9 %fusion.94 = bf16[12,64,256]{2,1,0:T(8,128)(2,1)S(1)} fusion(f32[12,256,1434]{1,2,0:T(8,128)} %get-tuple-element.488, f32[12,256]{1,0:T(8,128)} %get-tuple-element.489, bf16[1178,12,64]{0,2,1:T(8,128)(2,1)S(1)} %copy-done.1, bf16[256,12,64]{0,2,1:T(8,128)(2,1)S(1)} %bitcast.116), kind=kOutput, calls=%fused_computation.29.clone.1 | convolution fusion | flops 577284096 | bytes 20229120 | tf_op jit(solution)/shard_map/while/body/eval_jaxpr/hqk,khd->qhd/dot_general | solution.py:54
  266.3 2.7 fusion.95
  270.0 3.4 collective-permute-start
  286.2 6.1 %fusion.89 = bf16[256,2304]{0,1:T(8,128)(2,1)S(1)} fusion(bf16[1536,2304]{1,0:T(8,128)(2,1)} %get-tuple-element.539, bf16[256,1536]{1,0:T(8,128)(2,1)S(1)} %all_gather.16, f32[1536]{0:T(1024)S(1)} %get-tuple-element.484, f32[1536]{0:T(1024)S(1)} %get-tuple-element.485, f32[256]{0:T(256)S(1)} %add_rsqrt_fusion.2, f32[256]{0:T(256)S(1)} %broadcast_multiply_fusion.2), kind=kOutput, calls=%fused_computation.30.clone.1 | convolution fusion | flops 1814298624 | bytes 9058304 | tf_op jit(solution)/shard_map/while/body/eval_jaxpr/dot_general | solution.py:89
  292.5 8.5 %fusion.91 = f32[12,256,1434]{1,2,0:T(8,128)} fusion(bf16[1178,12,64]{0,2,1:T(8,128)(2,1)S(1)} %get-tuple-element.483, bf16[256,12,64]{0,2,1:T(8,128)(2,1)S(1)} %bitcast.112, bf16[256,12,1,64]{0,3,2,1:T(8,128)(2,1)S(1)} %get-tuple-element.487), kind=kOutput, calls=%fused_computation.14.clone.1 | convolution fusion | flops 568276992 | bytes 20216832 | tf_op jit(solution)/shard_map/while/body/eval_jaxpr/qhd,khd->hqk/dot_general | solution.py:42
  301.0 21.2 %fusion.93 = (f32[12,256]{1,0:T(8,128)}, f32[12,256,1434]{1,2,0:T(8,128)}) fusion(f32[12,256,1434]{1,2,0:T(8,128)} %fusion.91, pred[1434]{0:T(1024)(128)(4,1)S(1)} %fusion.92), kind=kOutput, calls=%fused_computation.102.clone.1 | output fusion | flops 26432920 | bytes 35255704 | tf_op jit(solution)/shard_map/while/body/eval_jaxpr/sub | solution.py:52
  322.2 7.9 %fusion.94 = bf16[12,64,256]{2,1,0:T(8,128)(2,1)S(1)} fusion(f32[12,256,1434]{1,2,0:T(8,128)} %get-tuple-element.488, f32[12,256]{1,0:T(8,128)} %get-tuple-element.489, bf16[1178,12,64]{0,2,1:T(8,128)(2,1)S(1)} %copy-done.1, bf16[256,12,64]{0,2,1:T(8,128)(2,1)S(1)} %bitcast.116), kind=kOutput, calls=%fused_computation.29.clone.1 | convolution fusion | flops 577284096 | bytes 20229120 | tf_op jit(solution)/shard_map/while/body/eval_jaxpr/hqk,khd->qhd/dot_general | solution.py:54
  337.1 5.0 %reduce-scatter.2.cloned.1.call-done = bf16[128,1536]{1,0:T(8,128)(2,1)} async-done(((bf16[256,1536]{1,0:T(8,128)(2,1)}), bf16[128,1536]{1,0:T(8,128)(2,1)}) %reduce-scatter.2.cloned.1.call-update) | async-done | bytes 393232 | tf_op jit(solution)/shard_map/while/body/eval_jaxpr/reduce_scatter | solution.py:120
  342.1 2.7 fusion.95
  345.8 3.6 collective-permute-start
  362.3 6.1 %fusion.89 = bf16[256,2304]{0,1:T(8,128)(2,1)S(1)} fusion(bf16[1536,2304]{1,0:T(8,128)(2,1)} %get-tuple-element.539, bf16[256,1536]{1,0:T(8,128)(2,1)S(1)} %all_gather.16, f32[1536]{0:T(1024)S(1)} %get-tuple-element.484, f32[1536]{0:T(1024)S(1)} %get-tuple-element.485, f32[256]{0:T(256)S(1)} %add_rsqrt_fusion.2, f32[256]{0:T(256)S(1)} %broadcast_multiply_fusion.2), kind=kOutput, calls=%fused_computation.30.clone.1 | convolution fusion | flops 1814298624 | bytes 9058304 | tf_op jit(solution)/shard_map/while/body/eval_jaxpr/dot_general | solution.py:89
  368.5 8.5 %fusion.91 = f32[12,256,1434]{1,2,0:T(8,128)} fusion(bf16[1178,12,64]{0,2,1:T(8,128)(2,1)S(1)} %get-tuple-element.483, bf16[256,12,64]{0,2,1:T(8,128)(2,1)S(1)} %bitcast.112, bf16[256,12,1,64]{0,3,2,1:T(8,128)(2,1)S(1)} %get-tuple-element.487), kind=kOutput, calls=%fused_computation.14.clone.1 | convolution fusion | flops 568276992 | bytes 20216832 | tf_op jit(solution)/shard_map/while/body/eval_jaxpr/qhd,khd->hqk/dot_general | solution.py:42
  377.0 21.2 %fusion.93 = (f32[12,256]{1,0:T(8,128)}, f32[12,256,1434]{1,2,0:T(8,128)}) fusion(f32[12,256,1434]{1,2,0:T(8,128)} %fusion.91, pred[1434]{0:T(1024)(128)(4,1)S(1)} %fusion.92), kind=kOutput, calls=%fused_computation.102.clone.1 | output fusion | flops 26432920 | bytes 35255704 | tf_op jit(solution)/shard_map/while/body/eval_jaxpr/sub | solution.py:52
  398.3 7.9 %fusion.94 = bf16[12,64,256]{2,1,0:T(8,128)(2,1)S(1)} fusion(f32[12,256,1434]{1,2,0:T(8,128)} %get-tuple-element.488, f32[12,256]{1,0:T(8,128)} %get-tuple-element.489, bf16[1178,12,64]{0,2,1:T(8,128)(2,1)S(1)} %copy-done.1, bf16[256,12,64]{0,2,1:T(8,128)(2,1)S(1)} %bitcast.116), kind=kOutput, calls=%fused_computation.29.clone.1 | convolution fusion | flops 577284096 | bytes 20229120 | tf_op jit(solution)/shard_map/while/body/eval_jaxpr/hqk,khd->qhd/dot_general | solution.py:54
  413.1 5.0 %reduce-scatter.2.cloned.1.call-done = bf16[128,1536]{1,0:T(8,128)(2,1)} async-done(((bf16[256,1536]{1,0:T(8,128)(2,1)}), bf16[128,1536]{1,0:T(8,128)(2,1)}) %reduce-scatter.2.cloned.1.call-update) | async-done | bytes 393232 | tf_op jit(solution)/shard_map/while/body/eval_jaxpr/reduce_scatter | solution.py:120
  418.2 2.7 fusion.95
  (126 shorter events, 74.5 us)
Async XLA Ops:
  7.2 147.7 %all-gather.3.cloned.1.call-start = ((), (), s32[]{:S(2)}) async-start(), calls=%async_computation.1 | async-start | bytes 2654208 | tf_op jit(solution)/shard_map/all_gather | solution.py:85
  7.2 25.9 %collective-permute-start.1 = (bf16[192,2304]{1,0:T(8,128)(2,1)}, bf16[192,2304]{1,0:T(8,128)(2,1)S(1)}, u32[]{:S(2)}, u32[]{:S(2)}) collective-permute-start(bf16[192,2304]{1,0:T(8,128)(2,1)} %bitcast.121), channel_id=1, source_target_pairs={{0,2},{2,4},{4,6},{6,8},{8,10},{10,12},{12,14},{14,0},{1,3},{3,5},... | collective-permute-start | bytes 2654216 | tf_op jit(solution)/shard_map/ppermute | solution.py:23
  33.1 23.5 %collective-permute-start.2 = (bf16[192,2304]{1,0:T(8,128)(2,1)S(1)}, bf16[192,2304]{1,0:T(8,128)(2,1)S(1)}, u32[]{:S(2)}, u32[]{:S(2)}) collective-permute-start(bf16[192,2304]{1,0:T(8,128)(2,1)S(1)} %collective-permute-done.1), channel_id=1, source_target_pairs={{0,2},{2,4},{4,6},{6,8},{8,10},{10,12},{12,14},{14,0},{1,3},{3,5},... | collective-permute-start | bytes 2654216 | tf_op jit(solution)/shard_map/ppermute | solution.py:23
  56.7 33.1 %collective-permute-start.3 = (bf16[192,2304]{1,0:T(8,128)(2,1)S(1)}, bf16[192,2304]{1,0:T(8,128)(2,1)S(1)}, u32[]{:S(2)}, u32[]{:S(2)}) collective-permute-start(bf16[192,2304]{1,0:T(8,128)(2,1)S(1)} %collective-permute-done.2), channel_id=1, source_target_pairs={{0,2},{2,4},{4,6},{6,8},{8,10},{10,12},{12,14},{14,0},{1,3},{3,5},... | collective-permute-start | bytes 2654216 | tf_op jit(solution)/shard_map/ppermute | solution.py:23
  59.3 30.4 %copy-start.2 = (bf16[1,192,2304]{2,1,0:T(8,128)(2,1)S(1)}, bf16[1,192,2304]{2,1,0:T(8,128)(2,1)}, u32[]{:S(2)}) copy-start(bf16[1,192,2304]{2,1,0:T(8,128)(2,1)} %param.12) | copy-start | bytes 2654212
  89.7 41.7 %collective-permute-start.4 = (bf16[192,2304]{1,0:T(8,128)(2,1)S(1)}, bf16[192,2304]{1,0:T(8,128)(2,1)S(1)}, u32[]{:S(2)}, u32[]{:S(2)}) collective-permute-start(bf16[192,2304]{1,0:T(8,128)(2,1)S(1)} %collective-permute-done.3), channel_id=1, source_target_pairs={{0,2},{2,4},{4,6},{6,8},{8,10},{10,12},{12,14},{14,0},{1,3},{3,5},... | collective-permute-start | bytes 2654216 | tf_op jit(solution)/shard_map/ppermute | solution.py:23
  131.4 21.5 %collective-permute-start.5 = (bf16[192,2304]{1,0:T(8,128)(2,1)S(1)}, bf16[192,2304]{1,0:T(8,128)(2,1)S(1)}, u32[]{:S(2)}, u32[]{:S(2)}) collective-permute-start(bf16[192,2304]{1,0:T(8,128)(2,1)S(1)} %collective-permute-done.4), channel_id=1, source_target_pairs={{0,2},{2,4},{4,6},{6,8},{8,10},{10,12},{12,14},{14,0},{1,3},{3,5},... | collective-permute-start | bytes 2654216 | tf_op jit(solution)/shard_map/ppermute | solution.py:23
  152.8 22.5 %collective-permute-start.6 = (bf16[192,2304]{1,0:T(8,128)(2,1)S(1)}, bf16[192,2304]{1,0:T(8,128)(2,1)S(1)}, u32[]{:S(2)}, u32[]{:S(2)}) collective-permute-start(bf16[192,2304]{1,0:T(8,128)(2,1)S(1)} %collective-permute-done.5), channel_id=1, source_target_pairs={{0,2},{2,4},{4,6},{6,8},{8,10},{10,12},{12,14},{14,0},{1,3},{3,5},... | collective-permute-start | bytes 2654216 | tf_op jit(solution)/shard_map/ppermute | solution.py:23
  175.4 15.7 %collective-permute-start.7 = (bf16[192,2304]{1,0:T(8,128)(2,1)S(1)}, bf16[192,2304]{1,0:T(8,128)(2,1)S(1)}, u32[]{:S(2)}, u32[]{:S(2)}) collective-permute-start(bf16[192,2304]{1,0:T(8,128)(2,1)S(1)} %collective-permute-done.6), channel_id=1, source_target_pairs={{0,2},{2,4},{4,6},{6,8},{8,10},{10,12},{12,14},{14,0},{1,3},{3,5},... | collective-permute-start | bytes 2654216 | tf_op jit(solution)/shard_map/ppermute | solution.py:23
  201.6 64.7 %reduce-scatter.2.cloned.1.call-start = ((), (), s32[]{:S(2)}) async-start(), calls=%async_computation.2 | async-start | bytes 1179648 | tf_op jit(solution)/shard_map/while/body/eval_jaxpr/reduce_scatter | solution.py:120
  201.7 9.7 %collective-permute-start = (bf16[128,1536]{1,0:T(8,128)(2,1)S(1)}, bf16[128,1536]{1,0:T(8,128)(2,1)S(1)}, u32[]{:S(2)}, u32[]{:S(2)}) collective-permute-start(bf16[128,1536]{1,0:T(8,128)(2,1)S(1)} %broadcast_select_fusion.4), channel_id=1, source_target_pairs={{0,16},{1,17},{2,18},{3,19},{4,20},{5,21},{6,22},{7,23},{8,24},{9,... | collective-permute-start | bytes 1179656 | tf_op jit(solution)/shard_map/while/body/eval_jaxpr/ppermute | solution.py:32
  230.2 21.2 %copy-start.1 = (bf16[1178,12,64]{0,2,1:T(8,128)(2,1)S(1)}, bf16[1178,12,64]{0,2,1:T(8,128)(2,1)}, u32[]{:S(2)}) copy-start(bf16[1178,12,64]{0,2,1:T(8,128)(2,1)} %get-tuple-element.490) | copy-start | bytes 5428228 | tf_op jit(solution)/shard_map/while
  251.4 7.9 %copy-start = (bf16[768,1536]{1,0:T(8,128)(2,1)S(1)}, bf16[768,1536]{1,0:T(8,128)(2,1)}, u32[]{:S(2)}) copy-start(bf16[768,1536]{1,0:T(8,128)(2,1)} %get-tuple-element.542) | copy-start | bytes 7077892 | tf_op jit(solution)/shard_map/while
  269.0 73.1 %reduce-scatter.2.cloned.1.call-start = ((), (), s32[]{:S(2)}) async-start(), calls=%async_computation.2 | async-start | bytes 1179648 | tf_op jit(solution)/shard_map/while/body/eval_jaxpr/reduce_scatter | solution.py:120
  270.0 12.3 %collective-permute-start = (bf16[128,1536]{1,0:T(8,128)(2,1)S(1)}, bf16[128,1536]{1,0:T(8,128)(2,1)S(1)}, u32[]{:S(2)}, u32[]{:S(2)}) collective-permute-start(bf16[128,1536]{1,0:T(8,128)(2,1)S(1)} %broadcast_select_fusion.4), channel_id=1, source_target_pairs={{0,16},{1,17},{2,18},{3,19},{4,20},{5,21},{6,22},{7,23},{8,24},{9,... | collective-permute-start | bytes 1179656 | tf_op jit(solution)/shard_map/while/body/eval_jaxpr/ppermute | solution.py:32
  301.0 21.2 %copy-start.1 = (bf16[1178,12,64]{0,2,1:T(8,128)(2,1)S(1)}, bf16[1178,12,64]{0,2,1:T(8,128)(2,1)}, u32[]{:S(2)}) copy-start(bf16[1178,12,64]{0,2,1:T(8,128)(2,1)} %get-tuple-element.490) | copy-start | bytes 5428228 | tf_op jit(solution)/shard_map/while
  322.2 7.9 %copy-start = (bf16[768,1536]{1,0:T(8,128)(2,1)S(1)}, bf16[768,1536]{1,0:T(8,128)(2,1)}, u32[]{:S(2)}) copy-start(bf16[768,1536]{1,0:T(8,128)(2,1)} %get-tuple-element.542) | copy-start | bytes 7077892 | tf_op jit(solution)/shard_map/while
  344.8 73.4 %reduce-scatter.2.cloned.1.call-start = ((), (), s32[]{:S(2)}) async-start(), calls=%async_computation.2 | async-start | bytes 1179648 | tf_op jit(solution)/shard_map/while/body/eval_jaxpr/reduce_scatter | solution.py:120
  345.8 12.5 %collective-permute-start = (bf16[128,1536]{1,0:T(8,128)(2,1)S(1)}, bf16[128,1536]{1,0:T(8,128)(2,1)S(1)}, u32[]{:S(2)}, u32[]{:S(2)}) collective-permute-start(bf16[128,1536]{1,0:T(8,128)(2,1)S(1)} %broadcast_select_fusion.4), channel_id=1, source_target_pairs={{0,16},{1,17},{2,18},{3,19},{4,20},{5,21},{6,22},{7,23},{8,24},{9,... | collective-permute-start | bytes 1179656 | tf_op jit(solution)/shard_map/while/body/eval_jaxpr/ppermute | solution.py:32
  377.0 21.2 %copy-start.1 = (bf16[1178,12,64]{0,2,1:T(8,128)(2,1)S(1)}, bf16[1178,12,64]{0,2,1:T(8,128)(2,1)}, u32[]{:S(2)}) copy-start(bf16[1178,12,64]{0,2,1:T(8,128)(2,1)} %get-tuple-element.490) | copy-start | bytes 5428228 | tf_op jit(solution)/shard_map/while
  398.3 7.9 %copy-start = (bf16[768,1536]{1,0:T(8,128)(2,1)S(1)}, bf16[768,1536]{1,0:T(8,128)(2,1)}, u32[]{:S(2)}) copy-start(bf16[768,1536]{1,0:T(8,128)(2,1)} %get-tuple-element.542) | copy-start | bytes 7077892 | tf_op jit(solution)/shard_map/while
Sparse Core Ops, SparseCore 0:
  56.8 70.7 all-gather.2
  261.1 4.9 reduce-scatter.1
  331.9 10.1 reduce-scatter.1
  408.0 10.1 reduce-scatter.1
